TPU v7x, 256 devices: a whole 4x4x8 slice. The times are simulated.
256 devices in a mesh: dp: 16 (over z, core), ctx: 4 (over x), head: 4 (over y).
Axes of the slice: x: 4, y: 4, z: 8, core: 2. Of those that a mesh axis runs over, the one named last changes fastest.
Arguments:
- hidden_in: bfloat16 [16, 2048, 8192], P('dp', 'ctx', 'head'), may hold values from -40 to 40
- w_query: bfloat16 [8192, 4096], P('dp', 'head'), may hold values from -0.0625 to 0.0625
- w_key: bfloat16 [8192, 512], P('dp', 'head'), may hold values from -0.0625 to 0.0625
- w_value: bfloat16 [8192, 512], P('dp', 'head'), may hold values from -0.0625 to 0.0625
- mem_gate: float32 [32], P('head'), may hold values from -3 to 3
Outputs:
- attended: bfloat16 [16, 2048, 4096], P('dp', 'ctx', 'head')
All inputs are finite; a program needn't handle non-finite values.
Results may differ from a plain program's by a relative error of at most 0.011.
Values may be sent and summed in bfloat16 or wider, within the bound.
A program may use at most 128 MiB of HBM per device.

v0:
```python
import math
import jax
import jax.numpy as jnp
from jax import lax
from jax.sharding import PartitionSpec as P

HD = 128
SEG = 128


def entering(shard, axis, combine, identity):
    peers, index = (lax.axis_size(axis), lax.axis_index(axis))
    everything = jax.tree.map(
        lambda part, kind: lax.all_gather(part.astype(kind), axis),
        shard,
        (jnp.bfloat16, jnp.bfloat16),
    )
    start = jax.tree.map(
        lambda part, zero: jnp.broadcast_to(jnp.asarray(zero, part.dtype), part.shape),
        shard,
        identity,
    )

    def lap(k, before):
        reached = k < index
        new = combine(
            before, jax.tree.map(lambda part, own: part[k].astype(own.dtype), everything, shard)
        )
        return jax.tree.map(lambda a, b: jnp.where(reached, a, b), new, before)

    return lax.fori_loop(0, peers, lap, start)


def feature_map(vector):
    return jax.nn.elu(vector) + 1.0


def exclusive_sum(stack):
    running = jnp.cumsum(stack, axis=0)
    return jnp.concatenate([jnp.zeros_like(stack[:1]), running[:-1]], axis=0)


def add_pair(earlier, later):
    return (earlier[0] + later[0], earlier[1] + later[1])


def body(hidden_in, w_query, w_key, w_value, mem_gate):
    highest = lax.Precision.HIGHEST
    features = lax.all_gather(hidden_in, "head", axis=2, tiled=True)
    tok_rows = features.shape[1]
    flattened = features[0]
    query_full = jnp.dot(
        flattened,
        lax.all_gather(w_query, "dp", axis=0, tiled=True),
        preferred_element_type=jnp.float32,
    )
    keys_full = jnp.dot(
        flattened,
        lax.all_gather(w_key, "dp", axis=0, tiled=True),
        preferred_element_type=jnp.float32,
    )
    values_full = jnp.dot(
        flattened,
        lax.all_gather(w_value, "dp", axis=0, tiled=True),
        preferred_element_type=jnp.float32,
    )
    query = query_full.astype(jnp.bfloat16)
    keys = keys_full.astype(jnp.bfloat16)
    values = values_full.astype(jnp.bfloat16)
    heads_dev = query.shape[1] // HD
    kv_dev = keys.shape[1] // HD
    group_size = heads_dev // kv_dev
    segments = tok_rows // SEG
    query_seg = query.reshape(segments, SEG, kv_dev, group_size, HD)
    key_seg = keys.reshape(segments, SEG, kv_dev, HD)
    value_seg = values.reshape(segments, SEG, kv_dev, HD)
    scores = jnp.einsum(
        "nqkgd,nskd->nkgqs", query_seg, key_seg, preferred_element_type=jnp.float32
    ) / math.sqrt(HD)
    causal = jnp.arange(SEG)[:, None] >= jnp.arange(SEG)[None, :]
    scores = jnp.where(causal, scores, -jnp.inf)
    probs = jax.nn.softmax(scores, axis=-1).astype(jnp.bfloat16)
    local = jnp.einsum("nkgqs,nskd->nqkgd", probs, value_seg, preferred_element_type=jnp.float32)
    value_wide = value_seg.astype(jnp.float32)
    feat_key = feature_map(key_seg.astype(jnp.float32))
    increment = jnp.einsum("nskd,nske->nkde", feat_key, value_wide, precision=highest)
    key_mass = jnp.sum(feat_key, axis=1)
    state_total = jnp.sum(increment, axis=0)
    mass_total = jnp.sum(key_mass, axis=0)
    prior_state, prior_mass = entering(
        (state_total, mass_total),
        "ctx",
        add_pair,
        (jnp.zeros_like(state_total), jnp.zeros_like(mass_total)),
    )
    memory = prior_state[None] + exclusive_sum(increment)
    mass_prior = prior_mass[None] + exclusive_sum(key_mass)
    feat_query = feature_map(query_seg.astype(jnp.float32))
    numerator = jnp.einsum("nqkgd,nkde->nqkge", feat_query, memory, precision=highest)
    denominator = jnp.einsum("nqkgd,nkd->nqkg", feat_query, mass_prior, precision=highest) + 1.0
    retrieved = numerator / denominator[..., None]
    gate_share = jax.nn.sigmoid(mem_gate).reshape(kv_dev, group_size)[None, None, :, :, None]
    mixed = gate_share * retrieved + (1.0 - gate_share) * local
    return mixed.reshape(1, tok_rows, heads_dev * HD).astype(jnp.bfloat16)


def solution(mesh):
    return jax.shard_map(
        body,
        mesh=mesh,
        in_specs=(
            P("dp", "ctx", "head"),
            P("dp", "head"),
            P("dp", "head"),
            P("dp", "head"),
            P("head"),
        ),
        out_specs=P("dp", "ctx", "head"),
        check_vma=False,
    )
```

profile of v0, /device:TPU:1, one launch (start us, length us, event | category | flops | bytes accessed | tf_op | source)
XLA Modules:
  0.0 307.1 jit_solution(8610718658696810357)
XLA Ops:
  6.5 0.7 all-gather.12.cloned.1.call-update
  7.3 0.7 all-gather.8.cloned.1.call-update
  8.1 0.7 all-gather.10.cloned.1.call-update
  8.8 0.5 all-gather.14.cloned.1.call-update
  9.4 43.4 %all-gather.12.cloned.1.call-done = bf16[8192,128]{1,0:T(8,128)(2,1)} async-done(((bf16[512,128]{1,0:T(8,128)(2,1)}), bf16[8192,128]{1,0:T(8,128)(2,1)}) %all-gather.12.cloned.1.call-update) | async-done | bytes 2097168 | tf_op jit(solution)/shard_map/all_gather | solution.py:64
  52.8 85.3 %all-gather.8.cloned.1.call-done = bf16[1,512,8192]{2,1,0:T(8,128)(2,1)} async-done(((bf16[1,512,2048]{2,1,0:T(8,128)(2,1)}), bf16[1,512,8192]{2,1,0:T(8,128)(2,1)}) %all-gather.8.cloned.1.call-update) | async-done | bytes 8388624 | tf_op jit(solution)/shard_map/all_gather | solution.py:49
  138.1 6.3 %fusion.24 = bf16[512,128]{1,0:T(8,128)(2,1)S(1)} fusion(bf16[8192,128]{1,0:T(8,128)(2,1)} %all-gather.12.cloned.1.call-done, bf16[1,512,8192]{2,1,0:T(8,128)(2,1)} %all-gather.8.cloned.1.call-done), kind=kOutput, calls=%fused_computation.27 | convolution fusion | flops 1073807360 | bytes 10616832 | tf_op jit(solution)/shard_map/dot_general | solution.py:62
  144.4 36.5 %all-gather.10.cloned.1.call-done = bf16[8192,128]{1,0:T(8,128)(2,1)} async-done(((bf16[512,128]{1,0:T(8,128)(2,1)}), bf16[8192,128]{1,0:T(8,128)(2,1)}) %all-gather.10.cloned.1.call-update) | async-done | bytes 2097168 | tf_op jit(solution)/shard_map/all_gather | solution.py:59
  180.9 6.3 %fusion.42 = (bf16[128]{0:T(256)(128)(2,1)S(1)}, bf16[512,128]{1,0:T(8,128)(2,1)S(1)}) fusion(bf16[8192,128]{1,0:T(8,128)(2,1)} %all-gather.10.cloned.1.call-done, bf16[1,512,8192]{2,1,0:T(8,128)(2,1)} %all-gather.8.cloned.1.call-done), kind=kOutput, calls=%fused_computation.48 | convolution fusion | flops 1074200448 | bytes 10617088 | tf_op jit(solution)/shard_map/dot_general | solution.py:57
  187.3 0.5 fusion.64
  187.7 0.2 fusion.47
  188.1 7.6 %all-gather.2 = bf16[4,1,128]{2,1,0:T(2,128)(2,1)S(1)} all-gather(bf16[1,1,128]{2,1,0:T(2,128)(2,1)S(1)} %bitcast.115), channel_id=3, replica_groups=mesh['dp'=16,'ctx'=4,'head'=4] {'ctx'}, dimensions={0}, use_global_device_ids=true | all-gather | bytes 1280 | tf_op jit(solution)/shard_map/all_gather | solution.py:14
  195.7 10.5 %all-gather = bf16[512,128]{1,0:T(8,128)(2,1)S(1)} all-gather(bf16[128,128]{1,0:T(8,128)(2,1)S(1)} %get-tuple-element.152), channel_id=2, replica_groups=mesh['dp'=16,'ctx'=4,'head'=4] {'ctx'}, dimensions={0}, use_global_device_ids=true | all-gather | bytes 163840 | tf_op jit(solution)/shard_map/all_gather | solution.py:14
  206.2 0.2 while.16
  206.4 70.0 %all-gather.14.cloned.1.call-done = bf16[8192,1024]{1,0:T(8,128)(2,1)} async-done(((bf16[512,1024]{1,0:T(8,128)(2,1)}), bf16[8192,1024]{1,0:T(8,128)(2,1)}) %all-gather.14.cloned.1.call-update) | async-done | bytes 16777232 | tf_op jit(solution)/shard_map/all_gather | solution.py:54
  276.4 14.8 %fusion.18 = bf16[64,8,8,128]{3,1,2,0:T(8,128)(2,1)S(1)} fusion(bf16[8192,1024]{1,0:T(8,128)(2,1)} %all-gather.14.cloned.1.call-done, bf16[1,512,8192]{2,1,0:T(8,128)(2,1)} %all-gather.8.cloned.1.call-done), kind=kOutput, calls=%fused_computation.25 | convolution fusion | flops 8590458880 | bytes 26214400 | tf_op jit(solution)/shard_map/dot_general | solution.py:52
  291.2 0.3 copy.37
  291.5 2.5 fusion.10
  294.1 2.8 fusion.12
  296.9 0.5 fusion.65
  297.3 0.4 fusion.14
  297.7 0.8 fusion.8
  298.5 0.7 copy.25
  299.3 1.3 convert_element_type.134
  (26 shorter events, 0.5 us)
Async XLA Ops:
  6.5 2.8 copy-start.1
  6.5 46.3 %all-gather.12.cloned.1.call-start = ((), (), s32[]{:S(2)}) async-start(), calls=%async_computation.2 | async-start | bytes 2228224 | tf_op jit(solution)/shard_map/all_gather | solution.py:64
  7.3 130.9 %all-gather.8.cloned.1.call-start = ((), (), s32[]{:S(2)}) async-start(), calls=%async_computation | async-start | bytes 10485760 | tf_op jit(solution)/shard_map/all_gather | solution.py:49
  8.0 172.9 %all-gather.10.cloned.1.call-start = ((), (), s32[]{:S(2)}) async-start(), calls=%async_computation.1 | async-start | bytes 2228224 | tf_op jit(solution)/shard_map/all_gather | solution.py:59
  8.7 267.7 %all-gather.14.cloned.1.call-start = ((), (), s32[]{:S(2)}) async-start(), calls=%async_computation.3 | async-start | bytes 17825792 | tf_op jit(solution)/shard_map/all_gather | solution.py:54
  187.9 103.3 %copy-start = (f32[4,1,128,128]{3,2,0,1:T(8,128)}, f32[4,1,128,128]{3,2,0,1:T(8,128)S(1)}, u32[]{:S(2)}) copy-start(f32[4,1,128,128]{3,2,0,1:T(8,128)S(1)} %fusion.47) | copy-start | bytes 786436
  291.5 2.5 slice-start
Sparse Core Ops, SparseCore 0:
  9.2 43.6 all-gather.11
  54.6 83.4 all-gather.7
  139.9 40.9 all-gather.9
  182.6 93.7 all-gather.13
where the time goes:
time: 307 us
  waiting for transfers between devices  238 us (78%)
  matrix products  34.5 us (11%)
  blocking collectives  18.1 us (6%)
  between operations  13.3 us (4%)
    all_gather x1, waiting for transfers between devices, body(): features = lax.all_gather(hidden_in, 'head', axis=2, tiled=True)  85.3 us
    all_gather x1, waiting for transfers between devices, body(): lax.all_gather(w_query, 'dp', axis=0, tiled=True)  70 us
    all_gather x1, waiting for transfers between devices, body(): lax.all_gather(w_value, 'dp', axis=0, tiled=True)  43.4 us
    all_gather x1, waiting for transfers between devices, body(): lax.all_gather(w_key, 'dp', axis=0, tiled=True)  36.5 us
    all_gather x2, blocking collectives, entering(): lax.all_gather(part.astype(kind), axis)  18.1 us
    dot_general x1, matrix products, body(): jnp.dot(flattened, lax.all_gather(w_query, 'dp', axis=0, tiled=True), pre...  14.8 us
    dot_general x1, matrix products, body(): jnp.dot(flattened, lax.all_gather(w_key, 'dp', axis=0, tiled=True), prefe...  6.33 us
    dot_general x1, matrix products, body(): jnp.dot(flattened, lax.all_gather(w_value, 'dp', axis=0, tiled=True), pre...  6.3 us
  transfers between devices with their start and end apart: 4, of which 4 were waited for; matrix products, arithmetic and copies ran while one was open for 4% of the time, Pallas kernels for 0%

commit v1 on v0

--- a/solution.py
+++ b/solution.py
@@ -6,6 +6,27 @@
 
 HD = 128
 SEG = 128
+
+
+def gather_around(x, axis, dim):
+    size, index, width = (lax.axis_size(axis), lax.axis_index(axis), x.shape[dim])
+    right = [(i, (i + 1) % size) for i in range(size)]
+    behind = [(i, (i - 1) % size) for i in range(size)]
+    out = jnp.zeros((*x.shape[:dim], size * width, *x.shape[dim + 1 :]), x.dtype)
+    out = lax.dynamic_update_slice_in_dim(out, x, index * width, axis=dim)
+    from_left = from_right = x
+    middle = size // 2
+    for step in range(1, middle + 1):
+        from_left = lax.ppermute(from_left, axis, right)
+        out = lax.dynamic_update_slice_in_dim(
+            out, from_left, (index - step) % size * width, axis=dim
+        )
+        if step < size - middle:
+            from_right = lax.ppermute(from_right, axis, behind)
+            out = lax.dynamic_update_slice_in_dim(
+                out, from_right, (index + step) % size * width, axis=dim
+            )
+    return out
 
 
 def entering(shard, axis, combine, identity):
@@ -60,9 +81,7 @@
         preferred_element_type=jnp.float32,
     )
     values_full = jnp.dot(
-        flattened,
-        lax.all_gather(w_value, "dp", axis=0, tiled=True),
-        preferred_element_type=jnp.float32,
+        flattened, gather_around(w_value, "dp", 0), preferred_element_type=jnp.float32
     )
     query = query_full.astype(jnp.bfloat16)
     keys = keys_full.astype(jnp.bfloat16)

time: 307 us -> 268 us (0.87)
  waiting for transfers between devices: 238 us -> 166 us
  starting transfers between devices: 0.12 us -> 31 us
    all_gather x1 -> x0, waiting for transfers between devices: 43.4 us -> none  [body(): lax.all_gather(w_value, 'dp', axis=0, tiled=True)]
    all_gather x1, waiting for transfers between devices: 85.3 us -> 45.7 us  [body(): features = lax.all_gather(hidden_in, 'head', axis=2, tiled=True)]
    ppermute x0 -> x15, starting transfers between devices: none -> 30.9 us  [the longest x7 23.6 us: gather_around(): from_right = lax.ppermute(from_right, axis, behind)]
    ppermute x0 -> x15, waiting for transfers between devices: none -> 11.9 us  [the longest x8 9.46 us: gather_around(): from_left = lax.ppermute(from_left, axis, right)]
  transfers between devices with their start and end apart: 4 -> 18, of which waited for: 4 -> 18; matrix products, arithmetic and copies ran while one was open for 4% -> 5% of each run, Pallas kernels for 0% -> 0%
where the time goes in v1:
time: 268 us
  waiting for transfers between devices  166 us (62%)
  matrix products  34.4 us (13%)
  starting transfers between devices  31 us (12%)
  blocking collectives  18.1 us (7%)
  between operations  13.7 us (5%)
  local copies, waits for them, and re-layouts  2.94 us (1%)
    all_gather x1, waiting for transfers between devices, body(): lax.all_gather(w_query, 'dp', axis=0, tiled=True)  70.1 us
    all_gather x1, waiting for transfers between devices, body(): features = lax.all_gather(hidden_in, 'head', axis=2, tiled=True)  45.7 us
    all_gather x1, waiting for transfers between devices, body(): lax.all_gather(w_key, 'dp', axis=0, tiled=True)  36.5 us
    ppermute x7, starting transfers between devices, gather_around(): from_right = lax.ppermute(from_right, axis, behind)  23.6 us
    all_gather x2, blocking collectives, entering(): lax.all_gather(part.astype(kind), axis)  18.1 us
    dot_general x1, matrix products, body(): jnp.dot(flattened, lax.all_gather(w_query, 'dp', axis=0, tiled=True), pre...  14.8 us
    ppermute x8, waiting for transfers between devices, gather_around(): from_left = lax.ppermute(from_left, axis, right)  9.46 us
    ppermute x8, starting transfers between devices, gather_around(): from_left = lax.ppermute(from_left, axis, right)  7.31 us
  transfers between devices with their start and end apart: 18, of which 18 were waited for; matrix products, arithmetic and copies ran while one was open for 5% of the time, Pallas kernels for 0%

profile of v1, /device:TPU:1, one launch (start us, length us, event | category | flops | bytes accessed | tf_op | source)
XLA Modules:
  0.0 267.5 jit_solution(837553691798934247)
XLA Ops:
  8.8 3.0 %collective-permute-start = (bf16[512,128]{1,0:T(8,128)(2,1)S(1)}, bf16[512,128]{1,0:T(8,128)(2,1)S(1)}, u32[]{:S(2)}, u32[]{:S(2)}) collective-permute-start(bf16[512,128]{1,0:T(8,128)(2,1)S(1)} %copy-done.1), channel_id=1, source_target_pairs={{0,16},{16,32},{32,48},{48,64},{64,80},{80,96},{96,112},{112,128},... | collective-permute-start | bytes 393224 | tf_op jit(solution)/shard_map/ppermute | solution.py:20
  12.7 1.0 collective-permute-done
  13.7 2.4 collective-permute-start.2
  16.5 1.7 collective-permute-start.3
  19.1 1.5 collective-permute-start.4
  20.9 3.0 %collective-permute-start.5 = (bf16[512,128]{1,0:T(8,128)(2,1)S(1)}, bf16[512,128]{1,0:T(8,128)(2,1)S(1)}, u32[]{:S(2)}, u32[]{:S(2)}) collective-permute-start(bf16[512,128]{1,0:T(8,128)(2,1)S(1)} %collective-permute-done.3), channel_id=1, source_target_pairs={{0,240},{16,0},{32,16},{48,32},{64,48},{80,64},{96,80},{112,96},{1... | collective-permute-start | bytes 393224 | tf_op jit(solution)/shard_map/ppermute | solution.py:25
  25.3 4.2 %collective-permute-start.7 = (bf16[512,128]{1,0:T(8,128)(2,1)S(1)}, bf16[512,128]{1,0:T(8,128)(2,1)S(1)}, u32[]{:S(2)}, u32[]{:S(2)}) collective-permute-start(bf16[512,128]{1,0:T(8,128)(2,1)S(1)} %collective-permute-done.5), channel_id=1, source_target_pairs={{0,240},{16,0},{32,16},{48,32},{64,48},{80,64},{96,80},{112,96},{1... | collective-permute-start | bytes 393224 | tf_op jit(solution)/shard_map/ppermute | solution.py:25
  30.4 4.6 %collective-permute-start.9 = (bf16[512,128]{1,0:T(8,128)(2,1)S(1)}, bf16[512,128]{1,0:T(8,128)(2,1)S(1)}, u32[]{:S(2)}, u32[]{:S(2)}) collective-permute-start(bf16[512,128]{1,0:T(8,128)(2,1)S(1)} %collective-permute-done.7), channel_id=1, source_target_pairs={{0,240},{16,0},{32,16},{48,32},{64,48},{80,64},{96,80},{112,96},{1... | collective-permute-start | bytes 393224 | tf_op jit(solution)/shard_map/ppermute | solution.py:25
  36.0 4.9 %collective-permute-start.11 = (bf16[512,128]{1,0:T(8,128)(2,1)S(1)}, bf16[512,128]{1,0:T(8,128)(2,1)S(1)}, u32[]{:S(2)}, u32[]{:S(2)}) collective-permute-start(bf16[512,128]{1,0:T(8,128)(2,1)S(1)} %collective-permute-done.9), channel_id=1, source_target_pairs={{0,240},{16,0},{32,16},{48,32},{64,48},{80,64},{96,80},{112,96},{1... | collective-permute-start | bytes 393224 | tf_op jit(solution)/shard_map/ppermute | solution.py:25
  41.9 5.0 %collective-permute-start.13 = (bf16[512,128]{1,0:T(8,128)(2,1)S(1)}, bf16[512,128]{1,0:T(8,128)(2,1)S(1)}, u32[]{:S(2)}, u32[]{:S(2)}) collective-permute-start(bf16[512,128]{1,0:T(8,128)(2,1)S(1)} %collective-permute-done.11), channel_id=1, source_target_pairs={{0,240},{16,0},{32,16},{48,32},{64,48},{80,64},{96,80},{112,96},{1... | collective-permute-start | bytes 393224 | tf_op jit(solution)/shard_map/ppermute | solution.py:25
  47.1 0.8 collective-permute-done.13
  47.9 4.7 %collective-permute-done.14 = bf16[512,128]{1,0:T(8,128)(2,1)S(1)} collective-permute-done((bf16[512,128]{1,0:T(8,128)(2,1)S(1)}, bf16[512,128]{1,0:T(8,128)(2,1)S(1)}, u32[]{:S(2)}, u32[]{:S(2)}) %collective-permute-start.14) | collective-permute-done | bytes 131104 | tf_op jit(solution)/shard_map/ppermute | solution.py:20
  52.7 45.7 %all-gather.7.cloned.1.call-done = bf16[1,512,8192]{2,1,0:T(8,128)(2,1)} async-done(((bf16[1,512,2048]{2,1,0:T(8,128)(2,1)}), bf16[1,512,8192]{2,1,0:T(8,128)(2,1)}) %all-gather.7.cloned.1.call-update) | async-done | bytes 8388624 | tf_op jit(solution)/shard_map/all_gather | solution.py:70
  98.4 6.3 %fusion.24 = bf16[128,512]{1,0:T(8,128)(2,1)S(1)} fusion(bf16[8192,128]{1,0:T(8,128)(2,1)S(1)} %constant_dynamic-update-slice_fusion, bf16[1,512,8192]{2,1,0:T(8,128)(2,1)} %all-gather.7.cloned.1.call-done), kind=kOutput, calls=%fused_computation.27 | convolution fusion | flops 1073807360 | bytes 10616832 | tf_op jit(solution)/shard_map/dot_general | solution.py:83
  104.7 36.5 %all-gather.9.cloned.1.call-done = bf16[8192,128]{1,0:T(8,128)(2,1)} async-done(((bf16[512,128]{1,0:T(8,128)(2,1)}), bf16[8192,128]{1,0:T(8,128)(2,1)}) %all-gather.9.cloned.1.call-update) | async-done | bytes 2097168 | tf_op jit(solution)/shard_map/all_gather | solution.py:80
  141.3 6.3 %fusion.42 = (bf16[128]{0:T(256)(128)(2,1)S(1)}, bf16[512,128]{1,0:T(8,128)(2,1)S(1)}) fusion(bf16[8192,128]{1,0:T(8,128)(2,1)} %all-gather.9.cloned.1.call-done, bf16[1,512,8192]{2,1,0:T(8,128)(2,1)} %all-gather.7.cloned.1.call-done), kind=kOutput, calls=%fused_computation.48 | convolution fusion | flops 1074200448 | bytes 10617088 | tf_op jit(solution)/shard_map/dot_general | solution.py:78
  148.4 7.6 %all-gather.2 = bf16[4,1,128]{2,1,0:T(2,128)(2,1)S(1)} all-gather(bf16[1,1,128]{2,1,0:T(2,128)(2,1)S(1)} %bitcast.123), channel_id=3, replica_groups=mesh['dp'=16,'ctx'=4,'head'=4] {'ctx'}, dimensions={0}, use_global_device_ids=true | all-gather | bytes 1280 | tf_op jit(solution)/shard_map/all_gather | solution.py:35
  156.1 10.5 %all-gather = bf16[512,128]{1,0:T(8,128)(2,1)S(1)} all-gather(bf16[128,128]{1,0:T(8,128)(2,1)S(1)} %get-tuple-element.152), channel_id=2, replica_groups=mesh['dp'=16,'ctx'=4,'head'=4] {'ctx'}, dimensions={0}, use_global_device_ids=true | all-gather | bytes 163840 | tf_op jit(solution)/shard_map/all_gather | solution.py:35
  166.8 70.1 %all-gather.11.cloned.1.call-done = bf16[8192,1024]{1,0:T(8,128)(2,1)} async-done(((bf16[512,1024]{1,0:T(8,128)(2,1)}), bf16[8192,1024]{1,0:T(8,128)(2,1)}) %all-gather.11.cloned.1.call-update) | async-done | bytes 16777232 | tf_op jit(solution)/shard_map/all_gather | solution.py:75
  236.9 14.8 %fusion.18 = bf16[64,8,8,128]{3,1,2,0:T(8,128)(2,1)S(1)} fusion(bf16[8192,1024]{1,0:T(8,128)(2,1)} %all-gather.11.cloned.1.call-done, bf16[1,512,8192]{2,1,0:T(8,128)(2,1)} %all-gather.7.cloned.1.call-done), kind=kOutput, calls=%fused_computation.25 | convolution fusion | flops 8590458880 | bytes 26214400 | tf_op jit(solution)/shard_map/dot_general | solution.py:73
  251.9 2.5 fusion.10
  254.5 2.8 %fusion.12 = f32[4,128,128,8]{2,1,3,0:T(8,128)S(1)} fusion(bf16[4,128,8,128]{3,2,1,0:T(8,128)(2,1)S(1)} %bitcast.111, f32[3,1,128,128]{3,2,0,1:T(8,128)S(1)} %slice-done, f32[128,128]{1,0:T(8,128)S(1)} %bitcast.113), kind=kOutput, calls=%fused_computation.22 | convolution fusion | flops 807993344 | bytes 3407872 | tf_op jit(solution)/shard_map/nqkgd,nkde->nqkge/dot_general | solution.py:118
  258.1 0.8 fusion.8
  259.7 1.3 convert_element_type.138
  (73 shorter events, 11.7 us)
Async XLA Ops:
  6.5 2.2 copy-start.1
  6.5 5.5 %copy-start.2 = (f32[8]{0:T(128)S(1)}, f32[8]{0:T(128)}, u32[]{:S(2)}) copy-start(f32[8]{0:T(128)} %param.11) | copy-start | bytes 100
  6.5 91.9 %all-gather.7.cloned.1.call-start = ((), (), s32[]{:S(2)}) async-start(), calls=%async_computation | async-start | bytes 10485760 | tf_op jit(solution)/shard_map/all_gather | solution.py:70
  7.3 134.0 %all-gather.9.cloned.1.call-start = ((), (), s32[]{:S(2)}) async-start(), calls=%async_computation.1 | async-start | bytes 2228224 | tf_op jit(solution)/shard_map/all_gather | solution.py:80
  8.0 228.9 %all-gather.11.cloned.1.call-start = ((), (), s32[]{:S(2)}) async-start(), calls=%async_computation.2 | async-start | bytes 17825792 | tf_op jit(solution)/shard_map/all_gather | solution.py:75
  8.8 5.0 %collective-permute-start = (bf16[512,128]{1,0:T(8,128)(2,1)S(1)}, bf16[512,128]{1,0:T(8,128)(2,1)S(1)}, u32[]{:S(2)}, u32[]{:S(2)}) collective-permute-start(bf16[512,128]{1,0:T(8,128)(2,1)S(1)} %copy-done.1), channel_id=1, source_target_pairs={{0,16},{16,32},{32,48},{48,64},{64,80},{80,96},{96,112},{112,128},... | collective-permute-start | bytes 393224 | tf_op jit(solution)/shard_map/ppermute | solution.py:20
  11.8 4.7 %collective-permute-start.1 = (bf16[512,128]{1,0:T(8,128)(2,1)S(1)}, bf16[512,128]{1,0:T(8,128)(2,1)S(1)}, u32[]{:S(2)}, u32[]{:S(2)}) collective-permute-start(bf16[512,128]{1,0:T(8,128)(2,1)S(1)} %copy-done.1), channel_id=1, source_target_pairs={{0,240},{16,0},{32,16},{48,32},{64,48},{80,64},{96,80},{112,96},{1... | collective-permute-start | bytes 393224 | tf_op jit(solution)/shard_map/ppermute | solution.py:25
  13.7 5.3 %collective-permute-start.2 = (bf16[512,128]{1,0:T(8,128)(2,1)S(1)}, bf16[512,128]{1,0:T(8,128)(2,1)S(1)}, u32[]{:S(2)}, u32[]{:S(2)}) collective-permute-start(bf16[512,128]{1,0:T(8,128)(2,1)S(1)} %collective-permute-done), channel_id=1, source_target_pairs={{0,16},{16,32},{32,48},{48,64},{64,80},{80,96},{96,112},{112,128},... | collective-permute-start | bytes 393224 | tf_op jit(solution)/shard_map/ppermute | solution.py:20
  16.5 4.4 %collective-permute-start.3 = (bf16[512,128]{1,0:T(8,128)(2,1)S(1)}, bf16[512,128]{1,0:T(8,128)(2,1)S(1)}, u32[]{:S(2)}, u32[]{:S(2)}) collective-permute-start(bf16[512,128]{1,0:T(8,128)(2,1)S(1)} %collective-permute-done.1), channel_id=1, source_target_pairs={{0,240},{16,0},{32,16},{48,32},{64,48},{80,64},{96,80},{112,96},{1... | collective-permute-start | bytes 393224 | tf_op jit(solution)/shard_map/ppermute | solution.py:25
  19.1 5.6 %collective-permute-start.4 = (bf16[512,128]{1,0:T(8,128)(2,1)S(1)}, bf16[512,128]{1,0:T(8,128)(2,1)S(1)}, u32[]{:S(2)}, u32[]{:S(2)}) collective-permute-start(bf16[512,128]{1,0:T(8,128)(2,1)S(1)} %collective-permute-done.2), channel_id=1, source_target_pairs={{0,16},{16,32},{32,48},{48,64},{64,80},{80,96},{96,112},{112,128},... | collective-permute-start | bytes 393224 | tf_op jit(solution)/shard_map/ppermute | solution.py:20
  20.9 4.4 %collective-permute-start.5 = (bf16[512,128]{1,0:T(8,128)(2,1)S(1)}, bf16[512,128]{1,0:T(8,128)(2,1)S(1)}, u32[]{:S(2)}, u32[]{:S(2)}) collective-permute-start(bf16[512,128]{1,0:T(8,128)(2,1)S(1)} %collective-permute-done.3), channel_id=1, source_target_pairs={{0,240},{16,0},{32,16},{48,32},{64,48},{80,64},{96,80},{112,96},{1... | collective-permute-start | bytes 393224 | tf_op jit(solution)/shard_map/ppermute | solution.py:25
  24.7 5.6 %collective-permute-start.6 = (bf16[512,128]{1,0:T(8,128)(2,1)S(1)}, bf16[512,128]{1,0:T(8,128)(2,1)S(1)}, u32[]{:S(2)}, u32[]{:S(2)}) collective-permute-start(bf16[512,128]{1,0:T(8,128)(2,1)S(1)} %collective-permute-done.4), channel_id=1, source_target_pairs={{0,16},{16,32},{32,48},{48,64},{64,80},{80,96},{96,112},{112,128},... | collective-permute-start | bytes 393224 | tf_op jit(solution)/shard_map/ppermute | solution.py:20
  25.3 5.2 %collective-permute-start.7 = (bf16[512,128]{1,0:T(8,128)(2,1)S(1)}, bf16[512,128]{1,0:T(8,128)(2,1)S(1)}, u32[]{:S(2)}, u32[]{:S(2)}) collective-permute-start(bf16[512,128]{1,0:T(8,128)(2,1)S(1)} %collective-permute-done.5), channel_id=1, source_target_pairs={{0,240},{16,0},{32,16},{48,32},{64,48},{80,64},{96,80},{112,96},{1... | collective-permute-start | bytes 393224 | tf_op jit(solution)/shard_map/ppermute | solution.py:25
  30.3 5.6 %collective-permute-start.8 = (bf16[512,128]{1,0:T(8,128)(2,1)S(1)}, bf16[512,128]{1,0:T(8,128)(2,1)S(1)}, u32[]{:S(2)}, u32[]{:S(2)}) collective-permute-start(bf16[512,128]{1,0:T(8,128)(2,1)S(1)} %collective-permute-done.6), channel_id=1, source_target_pairs={{0,16},{16,32},{32,48},{48,64},{64,80},{80,96},{96,112},{112,128},... | collective-permute-start | bytes 393224 | tf_op jit(solution)/shard_map/ppermute | solution.py:20
  30.4 5.6 %collective-permute-start.9 = (bf16[512,128]{1,0:T(8,128)(2,1)S(1)}, bf16[512,128]{1,0:T(8,128)(2,1)S(1)}, u32[]{:S(2)}, u32[]{:S(2)}) collective-permute-start(bf16[512,128]{1,0:T(8,128)(2,1)S(1)} %collective-permute-done.7), channel_id=1, source_target_pairs={{0,240},{16,0},{32,16},{48,32},{64,48},{80,64},{96,80},{112,96},{1... | collective-permute-start | bytes 393224 | tf_op jit(solution)/shard_map/ppermute | solution.py:25
  35.9 5.6 %collective-permute-start.10 = (bf16[512,128]{1,0:T(8,128)(2,1)S(1)}, bf16[512,128]{1,0:T(8,128)(2,1)S(1)}, u32[]{:S(2)}, u32[]{:S(2)}) collective-permute-start(bf16[512,128]{1,0:T(8,128)(2,1)S(1)} %collective-permute-done.8), channel_id=1, source_target_pairs={{0,16},{16,32},{32,48},{48,64},{64,80},{80,96},{96,112},{112,128},... | collective-permute-start | bytes 393224 | tf_op jit(solution)/shard_map/ppermute | solution.py:20
  36.0 5.9 %collective-permute-start.11 = (bf16[512,128]{1,0:T(8,128)(2,1)S(1)}, bf16[512,128]{1,0:T(8,128)(2,1)S(1)}, u32[]{:S(2)}, u32[]{:S(2)}) collective-permute-start(bf16[512,128]{1,0:T(8,128)(2,1)S(1)} %collective-permute-done.9), channel_id=1, source_target_pairs={{0,240},{16,0},{32,16},{48,32},{64,48},{80,64},{96,80},{112,96},{1... | collective-permute-start | bytes 393224 | tf_op jit(solution)/shard_map/ppermute | solution.py:25
  41.5 5.6 %collective-permute-start.12 = (bf16[512,128]{1,0:T(8,128)(2,1)S(1)}, bf16[512,128]{1,0:T(8,128)(2,1)S(1)}, u32[]{:S(2)}, u32[]{:S(2)}) collective-permute-start(bf16[512,128]{1,0:T(8,128)(2,1)S(1)} %collective-permute-done.10), channel_id=1, source_target_pairs={{0,16},{16,32},{32,48},{48,64},{64,80},{80,96},{96,112},{112,128},... | collective-permute-start | bytes 393224 | tf_op jit(solution)/shard_map/ppermute | solution.py:20
  41.9 6.0 %collective-permute-start.13 = (bf16[512,128]{1,0:T(8,128)(2,1)S(1)}, bf16[512,128]{1,0:T(8,128)(2,1)S(1)}, u32[]{:S(2)}, u32[]{:S(2)}) collective-permute-start(bf16[512,128]{1,0:T(8,128)(2,1)S(1)} %collective-permute-done.11), channel_id=1, source_target_pairs={{0,240},{16,0},{32,16},{48,32},{64,48},{80,64},{96,80},{112,96},{1... | collective-permute-start | bytes 393224 | tf_op jit(solution)/shard_map/ppermute | solution.py:25
  47.1 5.6 %collective-permute-start.14 = (bf16[512,128]{1,0:T(8,128)(2,1)S(1)}, bf16[512,128]{1,0:T(8,128)(2,1)S(1)}, u32[]{:S(2)}, u32[]{:S(2)}) collective-permute-start(bf16[512,128]{1,0:T(8,128)(2,1)S(1)} %collective-permute-done.12), channel_id=1, source_target_pairs={{0,16},{16,32},{32,48},{48,64},{64,80},{80,96},{96,112},{112,128},... | collective-permute-start | bytes 393224 | tf_op jit(solution)/shard_map/ppermute | solution.py:20
  148.2 103.4 %copy-start = (f32[4,1,128,128]{3,2,0,1:T(8,128)}, f32[4,1,128,128]{3,2,0,1:T(8,128)S(1)}, u32[]{:S(2)}) copy-start(f32[4,1,128,128]{3,2,0,1:T(8,128)S(1)} %fusion.47) | copy-start | bytes 786436
  251.9 2.5 slice-start
Sparse Core Ops, SparseCore 0:
  9.1 89.2 all-gather.6
  100.3 40.9 all-gather.8
  143.1 93.7 all-gather.10
